TPU v7x, 256 devices: a whole 4x4x8 slice. The times are simulated.
256 devices in a mesh: rows: 32 (over y, z), rhs: 8 (over x, core).
Axes of the slice: x: 4, y: 4, z: 8, core: 2. Of those that a mesh axis runs over, the one named last changes fastest.
Arguments:
- lower_panels: bfloat16 [131072, 1024], P('rows', 'rhs'), may hold values from -0.03125 to 0.03125
- parent_solution: bfloat16 [131072, 2048], P('rows', 'rhs'), may hold values from -6 to 6
- parent_rows: int32 [131072], P('rows'), may hold values from 0 to 131071, as said below
- live_counts: int32 [32], P('rows'), may hold values from 512 to 4096, as said below
- front_rhs: bfloat16 [1024, 2048], P('rows', 'rhs'), may hold values from -6 to 6
- coupling: float32 [512, 512], replicated, may hold values from -0.25 to 0.25
- inverse_one: float32 [512, 512], replicated, as said below
- inverse_two: float32 [512, 512], replicated, as said below
Outputs:
- solution: float32 [1024, 2048], P('rows', 'rhs')
Inputs may be any that keep to these rules, and one draw needn't show every extreme that they name: `parent_rows`: the 128 entries of an aligned block of one device's 4096 entries all lie among the 4096 rows of one index of rows, the block's owner; two blocks of one device have the same owner exactly when their block numbers differ by a multiple of 32. `live_counts`: the live rows of an index are its first ones. Each count is 4096 divided by 1, 2, 4 or 8, and some index has all 4096. `inverse_one`: upper triangular. `inverse_two`: upper triangular.
All inputs are finite; a program needn't handle non-finite values.
Results may differ from a plain program's by a relative error of at most 0.0003.
Values may be sent and summed in bfloat16 or wider, within the bound.
A program may use at most 64 MiB of HBM per device.

v0:
```python
import jax
import jax.numpy as jnp
from jax import lax
from jax.sharding import PartitionSpec as P

BLK = 128


def left_apply(matrix, right):
    return jnp.dot(
        matrix, right, precision=lax.Precision.HIGHEST, preferred_element_type=jnp.float32
    )


def body(
    lower_panels,
    parent_solution,
    parent_rows,
    live_counts,
    front_rhs,
    coupling,
    inverse_one,
    inverse_two,
):
    groups = lax.axis_size("rows")
    rows_dev = parent_rows.shape[0]
    block_count = rows_dev // BLK
    slot_count = (block_count + groups - 1) // groups
    columns_dev = parent_solution.shape[1]
    panel_width = inverse_one.shape[0]
    pivot_width = 2 * panel_width
    pivot_share = front_rhs.shape[0]
    start_own = lax.axis_index("rows") * pivot_share
    block_lists = parent_rows.reshape(block_count, BLK)
    owners = block_lists[:, 0] // rows_dev
    local_rows = block_lists - owners[:, None] * rows_dev
    slot_of = jnp.arange(block_count, dtype=jnp.int32) // groups
    requests = jnp.zeros((groups, slot_count, BLK), jnp.int32).at[owners, slot_of].set(local_rows)
    received = lax.all_to_all(requests, "rows", split_axis=0, concat_axis=0, tiled=True)
    picked = parent_solution[received.reshape(-1)].reshape(received.shape + (columns_dev,))
    returned = lax.all_to_all(picked, "rows", split_axis=0, concat_axis=0, tiled=True)
    fetched = returned[owners, slot_of].reshape(rows_dev, columns_dev)
    live_mask = jnp.arange(rows_dev, dtype=jnp.int32) < live_counts[0]
    values = jnp.where(live_mask[:, None], fetched, jnp.zeros((), fetched.dtype))
    rhs_float = front_rhs.astype(jnp.float32)
    placed = lax.dynamic_update_slice(
        jnp.zeros((pivot_width, columns_dev), jnp.float32), rhs_float, (start_own, 0)
    )
    product = lax.dot_general(
        lax.all_gather(lower_panels, "rhs", axis=1, tiled=True),
        values,
        (((0,), (0,)), ((), ())),
        preferred_element_type=jnp.float32,
    )
    shares = lax.psum_scatter(placed - product, "rows", scatter_dimension=0, tiled=True)
    residual = lax.all_gather(shares, "rows", axis=0, tiled=True)
    second = left_apply(inverse_two, residual[panel_width:])
    reduced = residual[:panel_width] - left_apply(coupling, second)
    first = left_apply(inverse_one, reduced)
    solved = jnp.concatenate([first, second], axis=0)
    return lax.dynamic_slice_in_dim(solved, start_own, pivot_share, 0)


def solution(mesh):
    return jax.shard_map(
        body,
        mesh=mesh,
        in_specs=(
            P("rows", "rhs"),
            P("rows", "rhs"),
            P("rows"),
            P("rows"),
            P("rows", "rhs"),
            P(),
            P(),
            P(),
        ),
        out_specs=P("rows", "rhs"),
        check_vma=False,
    )
```

profile of v0, /device:TPU:1, one launch (start us, length us, event | category | flops | bytes accessed | tf_op | source)
XLA Modules:
  0.0 419.4 jit_solution(2627903179569624096)
XLA Ops:
  6.5 0.0 copy-start
  6.5 0.0 all-gather.3.cloned.1.call-start
  6.5 0.7 all-gather.3.cloned.1.call-update
  7.3 0.9 fusion.14
  8.1 0.9 scatter_custom_fusion
  9.1 20.5 %all_to_all.10 = s32[32,1,128]{2,1,0:T(1,128)S(1)} all-to-all(s32[32,1,128]{2,1,0:T(1,128)S(1)} %bitcast.40), channel_id=1, replica_groups=mesh['rows'=32,'rhs'=8] {'rows'}, dimensions={0} | all-to-all | bytes 32768 | tf_op jit(solution)/shard_map/all_to_all | solution.py:39
  29.6 0.0 copy-done
  29.6 17.0 %gather_fusion = bf16[4096,256]{1,0:T(8,128)(2,1)} fusion(bf16[4096,256]{1,0:T(8,128)(2,1)S(1)} %copy-done, s32[4096]{0:T(1024)S(1)} %broadcast_clamp_fusion), kind=kCustom, calls=%fused_computation | custom fusion | bytes 4210688 | tf_op jit(solution)/shard_map/gather | solution.py:40
  46.6 4.9 %all-to-all-start.1 = ((bf16[32,1,128,256]{3,2,1,0:T(8,128)(2,1)}), bf16[32,1,128,256]{3,2,1,0:T(8,128)(2,1)}, u32[]{:S(2)}, u32[]{:S(2)}) async-start(bf16[32,1,128,256]{3,2,1,0:T(8,128)(2,1)} %bitcast.37), calls=%async_computation.1 | async-start | bytes 4194304 | tf_op jit(solution)/shard_map/all_to_all | solution.py:41
  51.6 0.0 reduce-scatter.4.cloned.1.call-start
  51.6 0.1 copy.21
  52.4 0.1 broadcast_in_dim.12
  52.5 1.1 dynamic_update_slice.3
  53.6 47.4 %all-to-all-done.1 = bf16[32,1,128,256]{3,2,1,0:T(8,128)(2,1)} async-done(((bf16[32,1,128,256]{3,2,1,0:T(8,128)(2,1)}), bf16[32,1,128,256]{3,2,1,0:T(8,128)(2,1)}, u32[]{:S(2)}, u32[]{:S(2)}) %all-to-all-start.1) | async-done | bytes 2097184 | tf_op jit(solution)/shard_map/all_to_all | solution.py:41
  101.0 3.6 gather_fusion.1
  104.5 2.9 bitcast_select_fusion
  107.5 7.4 %fusion = f32[1024,256]{0,1:T(8,128)} fusion(f32[1024,256]{0,1:T(8,128)S(1)} %dynamic_update_slice.3, bf16[4096,256]{1,0:T(8,128)(2,1)} %bitcast_select_fusion, bf16[4096,1024]{1,0:T(8,128)(2,1)} %all-gather.3.cloned.1.call-done), kind=kOutput, calls=%fused_computation.5 | convolution fusion | flops 2147745792 | bytes 12582912 | tf_op jit(solution)/shard_map/dot_general | solution.py:49
  114.8 2.5 copy.27
  117.4 0.0 reduce-scatter.4.cloned.1.call-update
  117.4 0.0 all-gather.5.cloned.1.call-start
  117.4 210.3 %reduce-scatter.4.cloned.1.call-done = f32[32,256]{1,0:T(8,128)} async-done(((f32[1024,256]{1,0:T(8,128)}), f32[32,256]{1,0:T(8,128)}) %reduce-scatter.4.cloned.1.call-update) | async-done | bytes 32784 | tf_op jit(solution)/shard_map/reduce_scatter | solution.py:55
  327.7 0.0 all-gather.5.cloned.1.call-update
  327.8 77.4 %all-gather.5.cloned.1.call-done = f32[1024,256]{1,0:T(8,128)} async-done(((f32[32,256]{1,0:T(8,128)}), f32[1024,256]{1,0:T(8,128)}) %all-gather.5.cloned.1.call-update) | async-done | bytes 1048592 | tf_op jit(solution)/shard_map/all_gather | solution.py:56
  405.2 1.1 slice.19
  406.3 0.2 copy.29
  406.5 0.0 copy-start.1
  406.5 0.0 copy-start.2
  406.5 3.4 fusion.2
  409.9 1.1 fusion.1
  411.0 1.1 convolution_bitcast_fusion.1
  412.1 0.1 fusion.4
  412.2 0.7 copy.26
  (8 shorter events, 0.0 us)
Async XLA Ops:
  6.5 23.1 %copy-start = (bf16[4096,256]{1,0:T(8,128)(2,1)S(1)}, bf16[4096,256]{1,0:T(8,128)(2,1)}, u32[]{:S(2)}) copy-start(bf16[4096,256]{1,0:T(8,128)(2,1)} %param.9) | copy-start | bytes 6291460
  6.5 100.9 %all-gather.3.cloned.1.call-start = ((), (), s32[]{:S(2)}) async-start(), calls=%async_computation.3 | async-start | bytes 9437184 | tf_op jit(solution)/shard_map/all_gather | solution.py:50
  46.6 5.0 %copy-start.3 = (bf16[32,256]{1,0:T(8,128)(2,1)S(1)}, bf16[32,256]{1,0:T(8,128)(2,1)}, u32[]{:S(2)}) copy-start(bf16[32,256]{1,0:T(8,128)(2,1)} %param.12) | copy-start | bytes 49156
  46.6 54.3 %all-to-all-start.1 = ((bf16[32,1,128,256]{3,2,1,0:T(8,128)(2,1)}), bf16[32,1,128,256]{3,2,1,0:T(8,128)(2,1)}, u32[]{:S(2)}, u32[]{:S(2)}) async-start(bf16[32,1,128,256]{3,2,1,0:T(8,128)(2,1)} %bitcast.37), calls=%async_computation.1 | async-start | bytes 4194304 | tf_op jit(solution)/shard_map/all_to_all | solution.py:41
  51.6 276.2 %reduce-scatter.4.cloned.1.call-start = ((), (), s32[]{:S(2)}) async-start(), calls=%async_computation.5 | async-start | bytes 1081344 | tf_op jit(solution)/shard_map/reduce_scatter | solution.py:55
  117.4 287.8 %all-gather.5.cloned.1.call-start = ((), (), s32[]{:S(2)}) async-start(), calls=%async_computation.4 | async-start | bytes 1081344 | tf_op jit(solution)/shard_map/all_gather | solution.py:56
  406.5 3.4 copy-start.1
  406.5 4.5 %copy-start.2 = (f32[512,512]{1,0:T(8,128)S(1)}, f32[512,512]{1,0:T(8,128)}, u32[]{:S(2)}) copy-start(f32[512,512]{1,0:T(8,128)} %param.14) | copy-start | bytes 3145732
Sparse Core Ops, SparseCore 0:
  9.2 60.1 all-gather.2
  117.5 210.1 reduce-scatter.3
  330.3 74.8 all-gather.4
where the time goes:
time: 424 us; the launch traced here: 419 us
  waiting for transfers between devices  336 us (79%)
  local copies, waits for them, and re-layouts  26.4 us (6%)
  blocking collectives  20.5 us (5%)
  between operations  13.9 us (3%)
  matrix products  12.8 us (3%)
  starting transfers between devices  4.99 us (1%)
  other arithmetic  4.92 us (1%)
    reduce_scatter x1, waiting for transfers between devices, body(): lax.psum_scatter(placed - product, 'rows', scatter_dimension=0, tiled=True)  210 us
    all_gather x1, waiting for transfers between devices, body(): residual = lax.all_gather(shares, 'rows', axis=0, tiled=True)  77.4 us
    all_to_all x1, waiting for transfers between devices, body(): lax.all_to_all(picked, 'rows', split_axis=0, concat_axis=0, tiled=True)  47.4 us
    all_to_all x1, blocking collectives, body(): lax.all_to_all(requests, 'rows', split_axis=0, concat_axis=0, tiled=True)  20.5 us
    gather x1, local copies, waits for them, and re-layouts, body(): parent_solution[received.reshape(-1)]  17 us
  transfers between devices with their start and end apart: 4, of which 3 were waited for; matrix products, arithmetic and copies ran while one was open for 6% of the time, Pallas kernels for 0%

commit v1 on v0

v1 whole, which is shorter than its diff:
```python
import functools

import jax
import jax.numpy as jnp
from jax import lax
from jax.experimental import pallas as pl
from jax.experimental.pallas import tpu as pltpu
from jax.sharding import PartitionSpec as P

BLK = 128
TILE = 128
PLANE = (4, 8)
RING = 4
GROUP = 4
MESH = pl.DeviceIdType.MESH


def offsets(plane):
    size_y, size_z = plane
    pairs = [(dy, dz) for dy in range(size_y) for dz in range(size_z)]
    return sorted(
        pairs, key=lambda p: (min(p[0], size_y - p[0]) + min(p[1], size_z - p[1]), p)
    )


def kernel(
    plane,
    blocks_ref,
    rows_ref,
    parent_ref,
    rhs_ref,
    coupling_hbm,
    inverse_one_hbm,
    inverse_two_hbm,
    out_ref,
    panels,
    row_buf,
    row_smem,
    staged,
    wide,
    picked,
    fetched,
    product,
    shares,
    coupling,
    inverse_one,
    inverse_two,
    solved,
    returned,
    turned,
    load_sem,
    smem_sem,
    self_sem,
    row_send,
    row_recv,
    blk_send,
    blk_recv,
    near_send,
    near_recv,
    far_send,
    far_recv,
    twin_send,
    twin_recv,
    sum_send,
    sum_recv,
    out_send,
    out_recv,
):
    size_y, size_z = plane
    count = size_y * size_z
    groups = count // GROUP
    offs = offsets(plane)
    me = lax.axis_index("rows")
    side = lax.axis_index("rhs")
    y, z = me // size_z, me % size_z
    x, core = side // 2, side % 2
    right = ((x + 1) % RING) * 2 + core
    left = ((x + RING - 1) % RING) * 2 + core
    opposite = ((x + 2) % RING) * 2 + core
    twin = x * 2 + (1 - core)

    def target(t):
        dy, dz = offs[t]
        return ((y + size_y - dy) % size_y) * size_z + (z + size_z - dz) % size_z

    def source(t):
        dy, dz = offs[t]
        return ((y + dy) % size_y) * size_z + (z + dz) % size_z

    def remote(src, dst, send, recv, **device):
        return pltpu.make_async_remote_copy(
            src_ref=src, dst_ref=dst, send_sem=send, recv_sem=recv,
            device_id=device, device_id_type=MESH,
        )

    barrier = pltpu.get_barrier_semaphore()
    for t in range(1, count):
        pl.semaphore_signal(barrier, inc=1, device_id={"rows": target(t)}, device_id_type=MESH)
    for other in (left, right, twin):
        pl.semaphore_signal(barrier, inc=1, device_id={"rhs": other}, device_id_type=MESH)

    loads = [
        pltpu.make_async_copy(parent_ref, staged, load_sem.at[0]),
        pltpu.make_async_copy(coupling_hbm, coupling, load_sem.at[1]),
        pltpu.make_async_copy(inverse_one_hbm, inverse_one, load_sem.at[2]),
        pltpu.make_async_copy(inverse_two_hbm, inverse_two, load_sem.at[3]),
    ]
    for load in loads:
        load.start()
    own_block = pltpu.make_async_copy(blocks_ref.at[me], panels.at[side, 0], self_sem.at[0])
    own_block.start()
    own_rows = pltpu.make_async_copy(rows_ref.at[me], row_buf.at[0], self_sem.at[1])
    own_rows.start()

    pl.semaphore_wait(barrier, count + 2)

    row_copies, blk_copies = [], []
    for t in range(1, count):
        copy = remote(rows_ref.at[target(t)], row_buf.at[t], row_send.at[t], row_recv.at[t], rows=target(t))
        copy.start()
        row_copies.append(copy)
    for t in range(1, count):
        copy = remote(
            blocks_ref.at[target(t)], panels.at[side, t], blk_send.at[t], blk_recv.at[t], rows=target(t)
        )
        copy.start()
        blk_copies.append(copy)

    def part(cls, g):
        return panels.at[cls, pl.ds(g * GROUP, GROUP)]

    def near(direction, cls, g):
        other = right if direction == 0 else left
        return remote(part(cls, g), part(cls, g), near_send.at[direction, g], near_recv.at[direction, g], rhs=other)

    def far(cls, g):
        other = right if g % 2 == 0 else left
        return remote(part(cls, g), part(cls, g), far_send.at[g], far_recv.at[g], rhs=other)

    def pair(slot, cls, g):
        return remote(part(cls, g), part(cls, g), twin_send.at[slot, g], twin_recv.at[slot, g], rhs=twin)

    loads[0].wait()
    depth = wide.shape[0]
    step = 256

    def widen(i, carry):
        at = pl.ds(pl.multiple_of(i * step, step), step)
        wide[at, :] = staged[at, :].astype(jnp.float32)
        return carry

    lax.fori_loop(0, depth // step, widen, 0)

    own_rows.wait()
    for copy in row_copies:
        copy.wait_recv()
    to_smem = pltpu.make_async_copy(row_buf, row_smem, smem_sem)
    to_smem.start()
    to_smem.wait()

    def gather(t):
        def eight(i, carry):
            for u in range(8):
                at = row_smem[t, 0, i * 8 + u]
                picked[pl.ds(i * 8 + u, 1), :] = wide[pl.ds(at, 1), :]
            return carry

        lax.fori_loop(0, BLK // 8, eight, 0)
        fetched[t] = picked[...].T.astype(jnp.bfloat16)

    def gather_group(g):
        def one(k, carry):
            gather(g * GROUP + k)
            return carry

        lax.fori_loop(0, GROUP, one, 0)

    for g in range(groups + 2):
        if g < groups:
            for t in range(g * GROUP, (g + 1) * GROUP):
                if t == 0:
                    own_block.wait()
                else:
                    blk_copies[t - 1].wait_recv()
            near(0, side, g).start()
            near(1, side, g).start()
            pair(0, side, g).start()
        if 1 <= g <= groups:
            near(0, left, g - 1).wait_recv()
            if (g - 1) % 2 == 0:
                far(left, g - 1).start()
            pair(1, left, g - 1).start()
            near(1, right, g - 1).wait_recv()
            if (g - 1) % 2 == 1:
                far(right, g - 1).start()
            pair(2, right, g - 1).start()
        if g >= 2:
            far(opposite, g - 2).wait_recv()
            pair(3, opposite, g - 2).start()
        if g < groups:
            gather_group(g)

    acc_cols = product.shape[0]
    chips = [x, (x + RING - 1) % RING, (x + 1) % RING, (x + 2) % RING]
    for slot, chip in enumerate(chips):
        for g in range(groups):
            pair(slot, chip * 2 + (1 - core), g).wait_recv()

        def accumulate(g, total, chip=chip):
            at = pl.ds(g * GROUP, GROUP)
            lhs = jnp.concatenate([fetched[g * GROUP + k] for k in range(GROUP)], axis=1)
            rhs = jnp.concatenate(
                [
                    panels[chip * 2, at].reshape(GROUP * BLK, TILE),
                    panels[chip * 2 + 1, at].reshape(GROUP * BLK, TILE),
                ],
                axis=1,
            )
            return total + jnp.dot(lhs, rhs, preferred_element_type=jnp.float32)

        lanes = pl.ds(pl.multiple_of(chip * 2 * TILE, 2 * TILE), 2 * TILE)
        product[:, lanes] = lax.fori_loop(
            0, groups, accumulate, jnp.zeros((acc_cols, 2 * TILE), jnp.float32)
        )

    share = rhs_ref.shape[0]
    spot = (me * share) % TILE
    place = (
        lax.broadcasted_iota(jnp.int32, (share, TILE), 0) + spot
        == lax.broadcasted_iota(jnp.int32, (share, TILE), 1)
    ).astype(jnp.bfloat16)
    placed = lax.dot_general(
        rhs_ref[...], place, (((0,), (0,)), ((), ())), preferred_element_type=jnp.float32
    )
    own_lanes = pl.ds(pl.multiple_of((me * share) // TILE * TILE, TILE), TILE)
    product[:, own_lanes] = product[:, own_lanes] - placed

    chunk = acc_cols // count

    def columns(index):
        return pl.ds(pl.multiple_of(index * chunk, chunk), chunk)

    sum_copies = []
    for t in range(1, count):
        copy = remote(product.at[columns(target(t))], shares.at[t], sum_send.at[t], sum_recv.at[t], rows=target(t))
        copy.start()
        sum_copies.append(copy)
    total = product[columns(me), :]
    for t in range(1, count):
        sum_copies[t - 1].wait_recv()
        total = total + shares[t]
    for load in loads[1:]:
        load.wait()

    def apply(right_rows, matrix):
        return lax.dot_general(
            right_rows, matrix, (((1,), (1,)), ((), ())),
            precision=lax.Precision.HIGHEST, preferred_element_type=jnp.float32,
        )

    half = inverse_one.shape[0]
    residual = -total
    second = apply(residual[:, half:], inverse_two[...])
    reduced = residual[:, :half] - apply(second, coupling[...])
    first = apply(reduced, inverse_one[...])
    for k in range(half // TILE):
        solved[k] = first[:, k * TILE : (k + 1) * TILE]
        solved[half // TILE + k] = second[:, k * TILE : (k + 1) * TILE]

    out_copies = []
    for t in range(1, count):
        to = target(t)
        copy = remote(
            solved.at[(to * share) // TILE], returned.at[me], out_send.at[t], out_recv.at[t], rows=to
        )
        copy.start()
        out_copies.append(copy)
    returned[me] = solved[(me * share) // TILE]
    for copy in out_copies:
        copy.wait_recv()
    turned[...] = returned[...].reshape(acc_cols, TILE).T
    out_ref[...] = turned[pl.ds(pl.multiple_of(spot, share), share), :]

    for copy in row_copies + blk_copies + sum_copies + out_copies:
        copy.wait_send()
    for g in range(groups):
        near(0, side, g).wait_send()
        near(1, side, g).wait_send()
        far(left if g % 2 == 0 else right, g).wait_send()
        for slot, cls in enumerate((side, left, right, opposite)):
            pair(slot, cls, g).wait_send()


def body(
    lower_panels,
    parent_solution,
    parent_rows,
    live_counts,
    front_rhs,
    coupling,
    inverse_one,
    inverse_two,
    plane=PLANE,
):
    count = plane[0] * plane[1]
    groups = count // GROUP
    rows_dev = parent_rows.shape[0]
    columns_dev = parent_solution.shape[1]
    panel_width = inverse_one.shape[0]
    pivots = 2 * panel_width
    classes = pivots // TILE
    lists = parent_rows.reshape(count, BLK)
    owners = lists[:, 0] // rows_dev
    index = jnp.arange(count, dtype=jnp.int32)
    block_of = jnp.sum(
        jnp.where(owners[None, :] == index[:, None], index[None, :], 0), axis=1, dtype=jnp.int32
    )
    rows = (lists % rows_dev)[block_of].reshape(count, 1, BLK)
    position = block_of[:, None] * BLK + jnp.arange(BLK, dtype=jnp.int32)[None, :]
    blocks = lower_panels.reshape(count, BLK, TILE)[block_of]
    blocks = jnp.where((position < live_counts[0])[:, :, None], blocks, jnp.zeros((), blocks.dtype))
    vmem = pl.BlockSpec(memory_space=pltpu.VMEM)
    anywhere = pl.BlockSpec(memory_space=pl.ANY)
    dma = pltpu.SemaphoreType.DMA
    f32, bf16 = jnp.float32, jnp.bfloat16
    return pl.pallas_call(
        functools.partial(kernel, plane),
        out_shape=jax.ShapeDtypeStruct((front_rhs.shape[0], columns_dev), f32),
        in_specs=[vmem, vmem, anywhere, vmem, anywhere, anywhere, anywhere],
        out_specs=vmem,
        scratch_shapes=[
            pltpu.VMEM((classes, count, BLK, TILE), bf16),
            pltpu.VMEM((count, 1, BLK), jnp.int32),
            pltpu.SMEM((count, 1, BLK), jnp.int32),
            pltpu.VMEM((rows_dev, columns_dev), bf16),
            pltpu.VMEM((rows_dev, columns_dev), f32),
            pltpu.VMEM((BLK, columns_dev), f32),
            pltpu.VMEM((count, columns_dev, BLK), bf16),
            pltpu.VMEM((columns_dev, pivots), f32),
            pltpu.VMEM((count, columns_dev // count, pivots), f32),
            pltpu.VMEM((panel_width, panel_width), f32),
            pltpu.VMEM((panel_width, panel_width), f32),
            pltpu.VMEM((panel_width, panel_width), f32),
            pltpu.VMEM((classes, columns_dev // count, TILE), f32),
            pltpu.VMEM((count, columns_dev // count, TILE), f32),
            pltpu.VMEM((TILE, columns_dev), f32),
            dma((4,)),
            dma,
            dma((2,)),
            dma((count,)),
            dma((count,)),
            dma((count,)),
            dma((count,)),
            dma((2, groups)),
            dma((2, groups)),
            dma((groups,)),
            dma((groups,)),
            dma((4, groups)),
            dma((4, groups)),
            dma((count,)),
            dma((count,)),
            dma((count,)),
            dma((count,)),
        ],
        compiler_params=pltpu.CompilerParams(
            collective_id=0, has_side_effects=True, vmem_limit_bytes=48 * 1024 * 1024
        ),
    )(blocks, rows, parent_solution, front_rhs, coupling, inverse_one, inverse_two)


def solution(mesh):
    return jax.shard_map(
        body,
        mesh=mesh,
        in_specs=(
            P("rows", "rhs"),
            P("rows", "rhs"),
            P("rows"),
            P("rows"),
            P("rows", "rhs"),
            P(),
            P(),
            P(),
        ),
        out_specs=P("rows", "rhs"),
        check_vma=False,
    )
```

time: 424 us -> 111 us (0.26)
  the two profiles are of different devices: /device:TPU:1 before, /device:TPU:2 now
where the time goes in v1:
time: 111 us
  Pallas kernels  103 us (93%)
  local copies, waits for them, and re-layouts  4.21 us (4%)
  other arithmetic  2.78 us (3%)
    pallas_call x1, Pallas kernels, body(): pl.pallas_call(functools.partial(kernel, plane), out_shape=jax.ShapeDtype...  103 us

profile of v1, /device:TPU:2, one launch (start us, length us, event | category | flops | bytes accessed | tf_op | source)
XLA Modules:
  0.0 111.1 jit_solution(1627201461421274467)
XLA Ops:
  0.0 0.0 copy-start
  0.7 0.5 copy-done
  1.2 0.8 slice_reduce_fusion
  2.1 0.1 select_reduce_fusion
  2.2 0.1 add_compare_fusion
  2.3 0.7 add_select_fusion
  3.0 0.6 gather_fusion.1
  3.6 0.0 copy-start.1
  3.6 0.0 copy-start.2
  3.6 0.0 copy-start.4
  3.6 1.7 %gather_fusion = bf16[32,128,128]{2,1,0:T(8,128)(2,1)} fusion(bf16[32,128,128]{2,1,0:T(8,128)(2,1)S(1)} %bitcast.10, s32[1024]{0:T(1024)S(1)} %pad_clamp_fusion), kind=kCustom, calls=%fused_computation | custom fusion | bytes 2097280 | tf_op jit(solution)/shard_map/gather | solution.py:320
  5.3 0.0 copy-start.3
  5.3 1.8 %broadcast_select_fusion.blocks_ref = bf16[32,128,128]{2,1,0:T(8,128)(2,1)S(1)} fusion(bf16[32,128,128]{2,1,0:T(8,128)(2,1)} %gather_fusion, pred[32,128]{1,0:T(8,128)(4,1)S(1)} %add_compare_fusion), kind=kLoop, calls=%fused_computation.2 | loop fusion | flops 524288 | bytes 2101248 | tf_op jit(solution)/shard_map/jit(_where)/select_n | solution.py:321
  7.2 0.0 copy-done.1
  7.2 0.0 copy-done.2
  7.2 0.0 copy-done.4
  7.2 0.0 copy-done.3
  7.2 103.3 %shard_map.82 = f32[32,256]{1,0:T(8,128)S(1)} custom-call(bf16[32,128,128]{2,1,0:T(8,128)(2,1)S(1)} %broadcast_select_fusion.blocks_ref, s32[32,1,128]{2,1,0:T(1,128)S(1)} %bitcast.11, bf16[4096,256]{1,0:T(8,128)(2,1)} %parent_ref.1, bf16[32,256]{1,0:T(8,128)(2,1)S(1)} %copy-done.4, f32[512,512]{1,0:T(8,128)S(1)} %copy-done.1, f32[512,512]{1,0:T(8,128)S(1)} %copy-done.2, ...), custom_call_target="tpu_custom_call" | custom-call | tf_op jit(solution)/shard_map/pallas_call | solution.py:326
  110.5 0.6 copy.11
  (4 shorter events, 0.0 us)
Async XLA Ops:
  0.0 1.2 %copy-start = (bf16[4096,128]{1,0:T(8,128)(2,1)S(1)}, bf16[4096,128]{1,0:T(8,128)(2,1)}, u32[]{:S(2)}) copy-start(bf16[4096,128]{1,0:T(8,128)(2,1)} %param.8) | copy-start | bytes 3145732
  3.6 3.6 %copy-start.1 = (f32[512,512]{1,0:T(8,128)S(1)}, f32[512,512]{1,0:T(8,128)}, u32[]{:S(2)}) copy-start(f32[512,512]{1,0:T(8,128)} %coupling_hbm.1) | copy-start | bytes 3145732
  3.6 3.6 %copy-start.2 = (f32[512,512]{1,0:T(8,128)S(1)}, f32[512,512]{1,0:T(8,128)}, u32[]{:S(2)}) copy-start(f32[512,512]{1,0:T(8,128)} %inverse_one_hbm.1) | copy-start | bytes 3145732
  3.6 3.6 %copy-start.4 = (bf16[32,256]{1,0:T(8,128)(2,1)S(1)}, bf16[32,256]{1,0:T(8,128)(2,1)}, u32[]{:S(2)}) copy-start(bf16[32,256]{1,0:T(8,128)(2,1)} %rhs_ref.1) | copy-start | bytes 49156
  5.3 1.9 %copy-start.3 = (f32[512,512]{1,0:T(8,128)S(1)}, f32[512,512]{1,0:T(8,128)}, u32[]{:S(2)}) copy-start(f32[512,512]{1,0:T(8,128)} %inverse_two_hbm.1) | copy-start | bytes 3145732

commit v2 on v1

v2 whole, which is shorter than its diff:
```python
import functools

import jax
import jax.numpy as jnp
from jax import lax
from jax.experimental import pallas as pl
from jax.experimental.pallas import tpu as pltpu
from jax.sharding import PartitionSpec as P

BLK = 128
TILE = 128
PLANE = (4, 8)
RING = 4
GROUP = 4
MESH = pl.DeviceIdType.MESH


def offsets(plane):
    size_y, size_z = plane
    pairs = [(dy, dz) for dy in range(size_y) for dz in range(size_z)]
    return sorted(
        pairs, key=lambda p: (min(p[1], size_z - p[1]), min(p[0], size_y - p[0]), p)
    )


def split(value):
    high = value.astype(jnp.bfloat16)
    low = (value - high.astype(jnp.float32)).astype(jnp.bfloat16)
    return high, low


def dot_split(left, right):
    def dot(a, b):
        return jnp.dot(a, b, preferred_element_type=jnp.float32)

    return dot(left[0], right[0]) + (dot(left[0], right[1]) + dot(left[1], right[0]))


def kernel(
    plane,
    blocks_ref,
    rows_ref,
    parent_ref,
    rhs_ref,
    coupling_hbm,
    inverse_one_hbm,
    inverse_two_hbm,
    out_ref,
    panels,
    row_buf,
    row_smem,
    staged,
    wide,
    picked,
    fetched,
    product,
    matrices,
    high,
    low,
    first_y,
    first_z,
    second_y,
    second_z,
    got_y,
    got_z,
    got_yz,
    got_zy,
    load_sem,
    smem_sem,
    self_sem,
    row_send,
    row_recv,
    blk_send,
    blk_recv,
    near_send,
    near_recv,
    far_send,
    far_recv,
    twin_send,
    twin_recv,
    y_send,
    y_recv,
    z_send,
    z_recv,
    yz_send,
    yz_recv,
    zy_send,
    zy_recv,
):
    size_y, size_z = plane
    count = size_y * size_z
    groups = count // GROUP
    offs = offsets(plane)
    me = lax.axis_index("rows")
    side = lax.axis_index("rhs")
    y, z = me // size_z, me % size_z
    x, core = side // 2, side % 2
    right = ((x + 1) % RING) * 2 + core
    left = ((x + RING - 1) % RING) * 2 + core
    opposite = ((x + 2) % RING) * 2 + core
    twin = x * 2 + (1 - core)

    def target(t):
        dy, dz = offs[t]
        return ((y + size_y - dy) % size_y) * size_z + (z + size_z - dz) % size_z

    def source(t):
        dy, dz = offs[t]
        return ((y + dy) % size_y) * size_z + (z + dz) % size_z

    def remote(src, dst, send, recv, **device):
        return pltpu.make_async_remote_copy(
            src_ref=src, dst_ref=dst, send_sem=send, recv_sem=recv,
            device_id=device, device_id_type=MESH,
        )

    barrier = pltpu.get_barrier_semaphore()
    for t in range(1, count):
        pl.semaphore_signal(barrier, inc=1, device_id={"rows": target(t)}, device_id_type=MESH)
    for other in (left, right, twin):
        pl.semaphore_signal(barrier, inc=1, device_id={"rhs": other}, device_id_type=MESH)

    loads = [
        pltpu.make_async_copy(parent_ref, staged, load_sem.at[0]),
        pltpu.make_async_copy(coupling_hbm, matrices.at[0], load_sem.at[1]),
        pltpu.make_async_copy(inverse_one_hbm, matrices.at[1], load_sem.at[2]),
        pltpu.make_async_copy(inverse_two_hbm, matrices.at[2], load_sem.at[3]),
    ]
    for load in loads:
        load.start()
    own_block = pltpu.make_async_copy(blocks_ref.at[me], panels.at[side, 0], self_sem.at[0])
    own_block.start()
    own_rows = pltpu.make_async_copy(rows_ref.at[me], row_buf.at[0], self_sem.at[1])
    own_rows.start()

    loads[0].wait()
    depth = staged.shape[0]
    step = 256

    def widen(i, carry):
        at = pl.ds(pl.multiple_of(i * step, step), step)
        wide[at, :] = staged[at, :].astype(jnp.float32)
        return carry

    lax.fori_loop(0, depth // step, widen, 0)
    wide[depth:, :] = jnp.zeros((wide.shape[0] - depth, wide.shape[1]), jnp.float32)

    pl.semaphore_wait(barrier, count + 2)

    row_copies, blk_copies = [], []
    for t in range(1, count):
        copy = remote(rows_ref.at[target(t)], row_buf.at[t], row_send.at[t], row_recv.at[t], rows=target(t))
        copy.start()
        row_copies.append(copy)
    for t in range(1, count):
        copy = remote(
            blocks_ref.at[target(t)], panels.at[side, t], blk_send.at[t], blk_recv.at[t], rows=target(t)
        )
        copy.start()
        blk_copies.append(copy)

    def part(cls, g):
        return panels.at[cls, pl.ds(g * GROUP, GROUP)]

    def near(direction, cls, g):
        other = right if direction == 0 else left
        return remote(part(cls, g), part(cls, g), near_send.at[direction, g], near_recv.at[direction, g], rhs=other)

    def far(cls, g):
        other = right if g % 2 == 0 else left
        return remote(part(cls, g), part(cls, g), far_send.at[g], far_recv.at[g], rhs=other)

    def pair(slot, cls, g):
        return remote(part(cls, g), part(cls, g), twin_send.at[slot, g], twin_recv.at[slot, g], rhs=twin)

    for load in loads[1:]:
        load.wait()
    for k in range(3):
        high[k], low[k] = split(matrices[k])

    own_rows.wait()
    for copy in row_copies:
        copy.wait_recv()
    to_smem = pltpu.make_async_copy(row_buf, row_smem, smem_sem)
    to_smem.start()
    to_smem.wait()

    def gather(t):
        def eight(i, carry):
            for u in range(8):
                at = row_smem[t, 0, i * 8 + u]
                picked[pl.ds(i * 8 + u, 1), :] = wide[pl.ds(at, 1), :]
            return carry

        lax.fori_loop(0, BLK // 8, eight, 0)
        fetched[t] = picked[...].T.astype(jnp.bfloat16)

    def gather_group(g):
        def one(k, carry):
            gather(g * GROUP + k)
            return carry

        lax.fori_loop(0, GROUP, one, 0)

    def from_side(g):
        near(0, left, g).wait_recv()
        if g % 2 == 0:
            far(left, g).start()
        pair(1, left, g).start()
        near(1, right, g).wait_recv()
        if g % 2 == 1:
            far(right, g).start()
        pair(2, right, g).start()

    def from_far(g):
        far(opposite, g).wait_recv()
        pair(3, opposite, g).start()

    for g in range(groups):
        for t in range(g * GROUP, (g + 1) * GROUP):
            if t == 0:
                own_block.wait()
            else:
                blk_copies[t - 1].wait_recv()
        near(0, side, g).start()
        near(1, side, g).start()
        pair(0, side, g).start()
        if g >= 2:
            from_side(g - 2)
        if g >= 5:
            from_far(g - 5)
        gather_group(g)
    for g in range(max(groups - 2, 0), groups):
        from_side(g)

    acc_cols = fetched.shape[1]
    chips = [x, (x + RING - 1) % RING, (x + 1) % RING, (x + 2) % RING]

    def multiply(slot, wait_each):
        chip = chips[slot]
        width = 2 * TILE

        def term(g):
            at = pl.ds(g * GROUP, GROUP)
            lhs = jnp.concatenate([fetched[g * GROUP + k] for k in range(GROUP)], axis=1)
            rhs = jnp.concatenate(
                [panels[chip * 2 + c, at].reshape(GROUP * BLK, TILE) for c in range(2)], axis=1
            )
            return jnp.dot(lhs, rhs, preferred_element_type=jnp.float32)

        if wait_each:
            total = jnp.zeros((acc_cols, width), jnp.float32)
            for g in range(groups):
                pair(slot, chip * 2 + (1 - core), g).wait_recv()
                total = total + term(g)
        else:
            for g in range(groups):
                pair(slot, chip * 2 + (1 - core), g).wait_recv()
            total = lax.fori_loop(
                0, groups, lambda g, s: s + term(g), jnp.zeros((acc_cols, width), jnp.float32)
            )
        product[pl.ds(pl.multiple_of(chip * width, width), width), :] = -total.T

    early = max(groups - 5, 0)
    multiply(0, False)
    for g in range(early, groups - 2):
        from_far(g)
    multiply(1, False)
    multiply(2, False)
    for g in range(max(groups - 2, early), groups):
        from_far(g)
    multiply(3, False)

    share = rhs_ref.shape[0]
    own = pl.ds(pl.multiple_of(me * share, share), share)
    product[own, :] = product[own, :] + rhs_ref[...].astype(jnp.float32)
    half = matrices.shape[1]
    units = share // 8
    stripes = units - 1

    def place(value, base):
        for r in range(half // share):
            index_y, index_z = divmod(base + r, size_z)
            for u in range(units):
                rows = value[r * share + u * 8 : r * share + u * 8 + 8]
                if u < stripes:
                    first_y[u, index_y, index_z] = rows
                else:
                    first_z[index_z, index_y] = rows

    second = dot_split((high[2], low[2]), split(product[half:, :]))
    place(second, half // share)
    reduced = product[:half, :] - dot_split((high[0], low[0]), split(second))
    place(dot_split((high[1], low[1]), split(reduced)), 0)

    y_copies, z_copies, yz_copies, zy_copies = [], [], [], []
    for u in range(stripes):
        for dy in range(1, size_y):
            to = (y + size_y - dy) % size_y
            copy = remote(
                first_y.at[u, to], got_y.at[u, dy - 1], y_send.at[u, dy - 1], y_recv.at[u, dy - 1],
                rows=to * size_z + z,
            )
            copy.start()
            y_copies.append(copy)
        if u == 0:
            for dz in range(1, size_z):
                to = (z + size_z - dz) % size_z
                copy = remote(
                    first_z.at[to], got_z.at[dz - 1], z_send.at[dz - 1], z_recv.at[dz - 1],
                    rows=y * size_z + to,
                )
                copy.start()
                z_copies.append(copy)

    def reduce_y(u):
        total = first_y[u, y]
        for dy in range(1, size_y):
            y_copies[u * (size_y - 1) + dy - 1].wait_recv()
            total = total + got_y[u, dy - 1]
        second_z[u] = total
        for dz in range(1, size_z):
            to = (z + size_z - dz) % size_z
            copy = remote(
                second_z.at[u, to], got_yz.at[u, dz - 1], yz_send.at[u, dz - 1], yz_recv.at[u, dz - 1],
                rows=y * size_z + to,
            )
            copy.start()
            yz_copies.append(copy)

    def reduce_z():
        total = first_z[z]
        for dz in range(1, size_z):
            z_copies[dz - 1].wait_recv()
            total = total + got_z[dz - 1]
        second_y[...] = total
        for dy in range(1, size_y):
            to = (y + size_y - dy) % size_y
            copy = remote(
                second_y.at[to], got_zy.at[dy - 1], zy_send.at[dy - 1], zy_recv.at[dy - 1],
                rows=to * size_z + z,
            )
            copy.start()
            zy_copies.append(copy)

    for u in range(stripes - 1):
        reduce_y(u)
    reduce_z()
    reduce_y(stripes - 1)
    for u in range(stripes):
        total = second_z[u, z]
        for dz in range(1, size_z):
            yz_copies[u * (size_z - 1) + dz - 1].wait_recv()
            total = total + got_yz[u, dz - 1]
        out_ref[u * 8 : u * 8 + 8, :] = total
    total = second_y[y]
    for copy, dy in zip(zy_copies, range(1, size_y)):
        copy.wait_recv()
        total = total + got_zy[dy - 1]
    out_ref[stripes * 8 :, :] = total

    for copy in row_copies + blk_copies + y_copies + z_copies + yz_copies + zy_copies:
        copy.wait_send()
    for g in range(groups):
        near(0, side, g).wait_send()
        near(1, side, g).wait_send()
        far(left if g % 2 == 0 else right, g).wait_send()
        for slot, cls in enumerate((side, left, right, opposite)):
            pair(slot, cls, g).wait_send()


def body(
    lower_panels,
    parent_solution,
    parent_rows,
    live_counts,
    front_rhs,
    coupling,
    inverse_one,
    inverse_two,
    plane=PLANE,
):
    count = plane[0] * plane[1]
    groups = count // GROUP
    rows_dev = parent_rows.shape[0]
    columns_dev = parent_solution.shape[1]
    panel_width = inverse_one.shape[0]
    pivots = 2 * panel_width
    classes = pivots // TILE
    lists = parent_rows.reshape(count, BLK)
    owners = lists[:, 0] // rows_dev
    index = jnp.arange(count, dtype=jnp.int32)
    block_of = jnp.sum(
        jnp.where(owners[None, :] == index[:, None], index[None, :], 0), axis=1, dtype=jnp.int32
    )
    position = block_of[:, None] * BLK + jnp.arange(BLK, dtype=jnp.int32)[None, :]
    rows = jnp.where(position < live_counts[0], (lists % rows_dev)[block_of], rows_dev)
    rows = rows.reshape(count, 1, BLK)
    blocks = lower_panels.reshape(count, BLK, TILE)[block_of]
    units = front_rhs.shape[0] // 8
    vmem = pl.BlockSpec(memory_space=pltpu.VMEM)
    anywhere = pl.BlockSpec(memory_space=pl.ANY)
    dma = pltpu.SemaphoreType.DMA
    f32, bf16 = jnp.float32, jnp.bfloat16
    return pl.pallas_call(
        functools.partial(kernel, plane),
        out_shape=jax.ShapeDtypeStruct((front_rhs.shape[0], columns_dev), f32),
        in_specs=[vmem, vmem, anywhere, vmem, anywhere, anywhere, anywhere],
        out_specs=vmem,
        scratch_shapes=[
            pltpu.VMEM((classes, count, BLK, TILE), bf16),
            pltpu.VMEM((count, 1, BLK), jnp.int32),
            pltpu.SMEM((count, 1, BLK), jnp.int32),
            pltpu.VMEM((rows_dev, columns_dev), bf16),
            pltpu.VMEM((rows_dev + 8, columns_dev), f32),
            pltpu.VMEM((BLK, columns_dev), f32),
            pltpu.VMEM((count, columns_dev, BLK), bf16),
            pltpu.VMEM((pivots, columns_dev), f32),
            pltpu.VMEM((3, panel_width, panel_width), f32),
            pltpu.VMEM((3, panel_width, panel_width), bf16),
            pltpu.VMEM((3, panel_width, panel_width), bf16),
            pltpu.VMEM((units - 1, plane[0], plane[1], 8, columns_dev), f32),
            pltpu.VMEM((plane[1], plane[0], 8, columns_dev), f32),
            pltpu.VMEM((plane[0], 8, columns_dev), f32),
            pltpu.VMEM((units - 1, plane[1], 8, columns_dev), f32),
            pltpu.VMEM((units - 1, plane[0] - 1, plane[1], 8, columns_dev), f32),
            pltpu.VMEM((plane[1] - 1, plane[0], 8, columns_dev), f32),
            pltpu.VMEM((units - 1, plane[1] - 1, 8, columns_dev), f32),
            pltpu.VMEM((plane[0] - 1, 8, columns_dev), f32),
            dma((4,)),
            dma,
            dma((2,)),
            dma((count,)),
            dma((count,)),
            dma((count,)),
            dma((count,)),
            dma((2, groups)),
            dma((2, groups)),
            dma((groups,)),
            dma((groups,)),
            dma((4, groups)),
            dma((4, groups)),
            dma((units - 1, plane[0] - 1)),
            dma((units - 1, plane[0] - 1)),
            dma((plane[1] - 1,)),
            dma((plane[1] - 1,)),
            dma((units - 1, plane[1] - 1)),
            dma((units - 1, plane[1] - 1)),
            dma((plane[0] - 1,)),
            dma((plane[0] - 1,)),
        ],
        compiler_params=pltpu.CompilerParams(
            collective_id=0, has_side_effects=True, vmem_limit_bytes=48 * 1024 * 1024
        ),
    )(blocks, rows, parent_solution, front_rhs, coupling, inverse_one, inverse_two)


def solution(mesh):
    return jax.shard_map(
        body,
        mesh=mesh,
        in_specs=(
            P("rows", "rhs"),
            P("rows", "rhs"),
            P("rows"),
            P("rows"),
            P("rows", "rhs"),
            P(),
            P(),
            P(),
        ),
        out_specs=P("rows", "rhs"),
        check_vma=False,
    )
```

time: 111 us -> 90.7 us (0.82)
  the two profiles are of different devices: /device:TPU:2 before, /device:TPU:1 now
where the time goes in v2:
time: 90.7 us; the launch traced here: 90.4 us
  Pallas kernels  82.9 us (91%)
  local copies, waits for them, and re-layouts  5.65 us (6%)
  other arithmetic  0.97 us (1%)
    pallas_call x1, Pallas kernels, body(): pl.pallas_call(functools.partial(kernel, plane), out_shape=jax.ShapeDtype...  82.9 us
    unnamed x11, local copies, waits for them, and re-layouts  3.5 us

profile of v2, /device:TPU:1, one launch (start us, length us, event | category | flops | bytes accessed | tf_op | source)
XLA Modules:
  0.0 90.4 jit_solution(16538238712988715327)
XLA Ops:
  0.0 0.0 copy-start
  0.0 0.0 copy-start.1
  0.0 0.0 copy-start.4
  0.8 0.4 copy-done
  1.2 0.8 slice_reduce_fusion
  2.1 0.1 select_reduce_fusion
  2.2 0.7 add_select_fusion
  3.0 0.6 gather_fusion.1
  3.5 0.1 compare_select_fusion.rows_ref
  3.6 0.7 gather_fusion
  4.4 0.0 copy-done.1
  4.4 0.0 copy-done.4
  4.4 0.0 copy-start.2
  4.4 1.2 %copy-done.2 = f32[512,512]{1,0:T(8,128)S(1)} copy-done((f32[512,512]{1,0:T(8,128)S(1)}, f32[512,512]{1,0:T(8,128)}, u32[]{:S(2)}) %copy-start.2) | copy-done | bytes 1048600
  5.7 0.0 copy-start.3
  5.7 1.2 %copy-done.3 = f32[512,512]{1,0:T(8,128)S(1)} copy-done((f32[512,512]{1,0:T(8,128)S(1)}, f32[512,512]{1,0:T(8,128)}, u32[]{:S(2)}) %copy-start.3) | copy-done | bytes 1048600
  6.9 82.9 %shard_map.82 = f32[32,256]{1,0:T(8,128)S(1)} custom-call(bf16[32,128,128]{2,1,0:T(8,128)(2,1)S(1)} %gather_fusion, s32[32,1,128]{2,1,0:T(1,128)S(1)} %compare_select_fusion.rows_ref, bf16[4096,256]{1,0:T(8,128)(2,1)} %parent_ref.1, bf16[32,256]{1,0:T(8,128)(2,1)S(1)} %copy-done.4, f32[512,512]{1,0:T(8,128)S(1)} %copy-done.1, f32[512,512]{1,0:T(8,128)S(1)} %copy-done.2, ...), custom_call_target="tpu_custom_call" | custom-call | tf_op jit(solution)/shard_map/pallas_call | solution.py:405
  89.8 0.6 copy.11
  (4 shorter events, 0.0 us)
Async XLA Ops:
  0.0 1.2 %copy-start = (bf16[4096,128]{1,0:T(8,128)(2,1)S(1)}, bf16[4096,128]{1,0:T(8,128)(2,1)}, u32[]{:S(2)}) copy-start(bf16[4096,128]{1,0:T(8,128)(2,1)} %param.8) | copy-start | bytes 3145732
  0.0 4.4 %copy-start.1 = (f32[512,512]{1,0:T(8,128)S(1)}, f32[512,512]{1,0:T(8,128)}, u32[]{:S(2)}) copy-start(f32[512,512]{1,0:T(8,128)} %coupling_hbm.1) | copy-start | bytes 3145732
  0.0 4.4 %copy-start.4 = (bf16[32,256]{1,0:T(8,128)(2,1)S(1)}, bf16[32,256]{1,0:T(8,128)(2,1)}, u32[]{:S(2)}) copy-start(bf16[32,256]{1,0:T(8,128)(2,1)} %rhs_ref.1) | copy-start | bytes 49156
  4.4 1.2 %copy-start.2 = (f32[512,512]{1,0:T(8,128)S(1)}, f32[512,512]{1,0:T(8,128)}, u32[]{:S(2)}) copy-start(f32[512,512]{1,0:T(8,128)} %inverse_one_hbm.1) | copy-start | bytes 3145732
  5.7 1.2 %copy-start.3 = (f32[512,512]{1,0:T(8,128)S(1)}, f32[512,512]{1,0:T(8,128)}, u32[]{:S(2)}) copy-start(f32[512,512]{1,0:T(8,128)} %inverse_two_hbm.1) | copy-start | bytes 3145732

commit v3 on v2

--- a/solution.py
+++ b/solution.py
@@ -38,14 +38,20 @@
 
 def kernel(
     plane,
-    blocks_ref,
-    rows_ref,
+    live_ref,
+    lists_ref,
+    lower_hbm,
     parent_ref,
     rhs_ref,
     coupling_hbm,
     inverse_one_hbm,
     inverse_two_hbm,
     out_ref,
+    order_buf,
+    order_ref,
+    held,
+    blocks_ref,
+    rows_ref,
     panels,
     row_buf,
     row_smem,
@@ -54,6 +60,7 @@
     picked,
     fetched,
     product,
+    partial,
     matrices,
     high,
     low,
@@ -67,7 +74,6 @@
     got_zy,
     load_sem,
     smem_sem,
-    self_sem,
     row_send,
     row_recv,
     blk_send,
@@ -125,13 +131,32 @@
         pltpu.make_async_copy(coupling_hbm, matrices.at[0], load_sem.at[1]),
         pltpu.make_async_copy(inverse_one_hbm, matrices.at[1], load_sem.at[2]),
         pltpu.make_async_copy(inverse_two_hbm, matrices.at[2], load_sem.at[3]),
+        pltpu.make_async_copy(lower_hbm, held, load_sem.at[4]),
     ]
-    for load in loads:
+    loads[4].start()
+    for load in loads[:4]:
         load.start()
-    own_block = pltpu.make_async_copy(blocks_ref.at[me], panels.at[side, 0], self_sem.at[0])
-    own_block.start()
-    own_rows = pltpu.make_async_copy(rows_ref.at[me], row_buf.at[0], self_sem.at[1])
-    own_rows.start()
+    rows_dev = staged.shape[0]
+    lane = lax.broadcasted_iota(jnp.int32, (1, BLK), 1)
+    owner = lax.div(lists_ref[:, 0:1], jnp.int32(rows_dev))
+    number = lax.broadcasted_iota(jnp.int32, (count, BLK), 0)
+    order_buf[...] = jnp.max(jnp.where(owner == lane, number, 0), axis=0, keepdims=True)
+    to_order = pltpu.make_async_copy(order_buf, order_ref, smem_sem.at[1])
+    to_order.start()
+    to_order.wait()
+    loads[4].wait()
+
+    def arrange(index, carry):
+        block = order_ref[0, index]
+        blocks_ref[index] = held[block]
+        alive = lane + block * BLK < live_ref[0]
+        local = lax.rem(lists_ref[pl.ds(block, 1), :], jnp.int32(rows_dev))
+        rows_ref[index] = jnp.where(alive, local, rows_dev)
+        return carry
+
+    lax.fori_loop(0, count, arrange, 0)
+    panels[side, 0] = blocks_ref[me]
+    row_buf[0] = rows_ref[me]
 
     loads[0].wait()
     depth = staged.shape[0]
@@ -173,17 +198,12 @@
     def pair(slot, cls, g):
         return remote(part(cls, g), part(cls, g), twin_send.at[slot, g], twin_recv.at[slot, g], rhs=twin)
 
-    for load in loads[1:]:
-        load.wait()
-    for k in range(3):
-        high[k], low[k] = split(matrices[k])
-
-    own_rows.wait()
-    for copy in row_copies:
-        copy.wait_recv()
-    to_smem = pltpu.make_async_copy(row_buf, row_smem, smem_sem)
-    to_smem.start()
-    to_smem.wait()
+    def take_rows():
+        for copy in row_copies:
+            copy.wait_recv()
+        to_smem = pltpu.make_async_copy(row_buf, row_smem, smem_sem.at[0])
+        to_smem.start()
+        to_smem.wait()
 
     def gather(t):
         def eight(i, carry):
@@ -202,96 +222,128 @@
 
         lax.fori_loop(0, GROUP, one, 0)
 
-    def from_side(g):
-        near(0, left, g).wait_recv()
-        if g % 2 == 0:
-            far(left, g).start()
-        pair(1, left, g).start()
-        near(1, right, g).wait_recv()
-        if g % 2 == 1:
-            far(right, g).start()
-        pair(2, right, g).start()
-
-    def from_far(g):
-        far(opposite, g).wait_recv()
-        pair(3, opposite, g).start()
-
-    for g in range(groups):
+    acc_cols = fetched.shape[1]
+    width = 2 * TILE
+    chips = [x, (x + RING - 1) % RING, (x + 1) % RING, (x + 2) % RING]
+    half = matrices.shape[1]
+
+    def forward(g):
         for t in range(g * GROUP, (g + 1) * GROUP):
-            if t == 0:
-                own_block.wait()
-            else:
+            if t > 0:
                 blk_copies[t - 1].wait_recv()
         near(0, side, g).start()
         near(1, side, g).start()
         pair(0, side, g).start()
-        if g >= 2:
+
+    def from_side(g):
+        near(0, left, g).wait_recv()
+        pair(1, left, g).start()
+        near(1, right, g).wait_recv()
+        pair(2, right, g).start()
+
+    def relay(g):
+        far(left if g % 2 == 0 else right, g).start()
+
+    def from_far(g):
+        far(opposite, g).wait_recv()
+        pair(3, opposite, g).start()
+
+    def term(slot, g):
+        chip = chips[slot]
+        pair(slot, chip * 2 + (1 - core), g).wait_recv()
+        at = pl.ds(g * GROUP, GROUP)
+        lhs = jnp.concatenate([fetched[g * GROUP + k] for k in range(GROUP)], axis=1)
+        rhs = jnp.concatenate(
+            [panels[chip * 2 + c, at].reshape(GROUP * BLK, TILE) for c in range(2)], axis=1
+        )
+        value = jnp.dot(lhs, rhs, preferred_element_type=jnp.float32)
+        partial[slot] = value if g == 0 else partial[slot] + value
+
+    def put(rows, columns, value):
+        top, bottom = split(value)
+        high[rows, columns] = top
+        low[rows, columns] = bottom
+
+    upper, lower = slice(0, half), slice(half, 2 * half)
+
+    def invert(stage):
+        if stage == 0:
+            for load in loads[1:4]:
+                load.wait()
+            put(upper, upper, matrices[1])
+            put(lower, lower, matrices[2])
+            put(lower, upper, matrices[0])
+        if stage == 1:
+            put(upper, lower, dot_split(
+                (high[lower, upper], low[lower, upper]), (high[lower, lower], low[lower, lower])
+            ))
+        if stage == 2:
+            put(upper, lower, -dot_split(
+                (high[upper, upper], low[upper, upper]), (high[upper, lower], low[upper, lower])
+            ))
+            high[lower, upper] = jnp.zeros((half, half), jnp.bfloat16)
+            low[lower, upper] = jnp.zeros((half, half), jnp.bfloat16)
+
+    for g in range(groups + 4):
+        if g == groups - 1:
+            relay(0)
+            relay(1)
+        if g < groups:
+            forward(g)
+        if g == 1:
+            take_rows()
+        if 2 <= g < groups + 2:
             from_side(g - 2)
-        if g >= 5:
-            from_far(g - 5)
-        gather_group(g)
-    for g in range(max(groups - 2, 0), groups):
-        from_side(g)
-
-    acc_cols = fetched.shape[1]
-    chips = [x, (x + RING - 1) % RING, (x + 1) % RING, (x + 2) % RING]
-
-    def multiply(slot, wait_each):
-        chip = chips[slot]
-        width = 2 * TILE
-
-        def term(g):
-            at = pl.ds(g * GROUP, GROUP)
-            lhs = jnp.concatenate([fetched[g * GROUP + k] for k in range(GROUP)], axis=1)
-            rhs = jnp.concatenate(
-                [panels[chip * 2 + c, at].reshape(GROUP * BLK, TILE) for c in range(2)], axis=1
-            )
-            return jnp.dot(lhs, rhs, preferred_element_type=jnp.float32)
-
-        if wait_each:
-            total = jnp.zeros((acc_cols, width), jnp.float32)
-            for g in range(groups):
-                pair(slot, chip * 2 + (1 - core), g).wait_recv()
-                total = total + term(g)
-        else:
-            for g in range(groups):
-                pair(slot, chip * 2 + (1 - core), g).wait_recv()
-            total = lax.fori_loop(
-                0, groups, lambda g, s: s + term(g), jnp.zeros((acc_cols, width), jnp.float32)
-            )
-        product[pl.ds(pl.multiple_of(chip * width, width), width), :] = -total.T
-
-    early = max(groups - 5, 0)
-    multiply(0, False)
-    for g in range(early, groups - 2):
+        if g >= groups:
+            for k in range(2 if g == groups else groups - 2 if g == groups + 1 else groups,
+                           groups - 2 if g == groups else groups if g == groups + 1 else groups):
+                relay(k)
+        if 1 <= g <= groups:
+            gather_group(g - 1)
+        if g == groups - 4:
+            invert(0)
+        if g == groups - 3:
+            invert(1)
+        if g == groups - 2:
+            invert(2)
+        if 3 <= g < groups + 3:
+            term(0, g - 3)
+        if g >= 4:
+            term(1, g - 4)
+            term(2, g - 4)
+
+    def pivots(slot):
+        return pl.ds(pl.multiple_of(chips[slot] * width, width), width)
+
+    for g in range(groups // 2):
         from_far(g)
-    multiply(1, False)
-    multiply(2, False)
-    for g in range(max(groups - 2, early), groups):
-        from_far(g)
-    multiply(3, False)
-
     share = rhs_ref.shape[0]
     own = pl.ds(pl.multiple_of(me * share, share), share)
+    for slot in range(3):
+        product[pivots(slot), :] = -partial[slot].T
+    product[pivots(3), :] = jnp.zeros((width, acc_cols), jnp.float32)
     product[own, :] = product[own, :] + rhs_ref[...].astype(jnp.float32)
-    half = matrices.shape[1]
+    product[...] = dot_split((high[...], low[...]), split(product[...]))
+    for g in range(groups // 2):
+        term(3, g)
+    for g in range(groups // 2, groups):
+        from_far(g)
+        if g > groups // 2:
+            term(3, g - 1)
+    term(3, groups - 1)
+
     units = share // 8
     stripes = units - 1
-
-    def place(value, base):
-        for r in range(half // share):
-            index_y, index_z = divmod(base + r, size_z)
-            for u in range(units):
-                rows = value[r * share + u * 8 : r * share + u * 8 + 8]
-                if u < stripes:
-                    first_y[u, index_y, index_z] = rows
-                else:
-                    first_z[index_z, index_y] = rows
-
-    second = dot_split((high[2], low[2]), split(product[half:, :]))
-    place(second, half // share)
-    reduced = product[:half, :] - dot_split((high[0], low[0]), split(second))
-    place(dot_split((high[1], low[1]), split(reduced)), 0)
+    last = dot_split((high[:, pivots(3)], low[:, pivots(3)]), split(-partial[3].T))
+    answer = product[...] + last
+    for r in range(count):
+        index_y, index_z = divmod(r, size_z)
+        for u in range(units):
+            rows = answer[r * share + u * 8 : r * share + u * 8 + 8]
+            if u < stripes:
+                first_y[u, index_y, index_z] = rows
+            else:
+                first_z[index_z, index_y] = rows
 
     y_copies, z_copies, yz_copies, zy_copies = [], [], [], []
     for u in range(stripes):
@@ -387,27 +439,23 @@
     panel_width = inverse_one.shape[0]
     pivots = 2 * panel_width
     classes = pivots // TILE
-    lists = parent_rows.reshape(count, BLK)
-    owners = lists[:, 0] // rows_dev
-    index = jnp.arange(count, dtype=jnp.int32)
-    block_of = jnp.sum(
-        jnp.where(owners[None, :] == index[:, None], index[None, :], 0), axis=1, dtype=jnp.int32
-    )
-    position = block_of[:, None] * BLK + jnp.arange(BLK, dtype=jnp.int32)[None, :]
-    rows = jnp.where(position < live_counts[0], (lists % rows_dev)[block_of], rows_dev)
-    rows = rows.reshape(count, 1, BLK)
-    blocks = lower_panels.reshape(count, BLK, TILE)[block_of]
     units = front_rhs.shape[0] // 8
     vmem = pl.BlockSpec(memory_space=pltpu.VMEM)
-    anywhere = pl.BlockSpec(memory_space=pl.ANY)
+    smem = pl.BlockSpec(memory_space=pltpu.SMEM)
+    hbm = pl.BlockSpec(memory_space=pltpu.HBM)
     dma = pltpu.SemaphoreType.DMA
     f32, bf16 = jnp.float32, jnp.bfloat16
     return pl.pallas_call(
         functools.partial(kernel, plane),
         out_shape=jax.ShapeDtypeStruct((front_rhs.shape[0], columns_dev), f32),
-        in_specs=[vmem, vmem, anywhere, vmem, anywhere, anywhere, anywhere],
+        in_specs=[smem, vmem, hbm, hbm, vmem, hbm, hbm, hbm],
         out_specs=vmem,
         scratch_shapes=[
+            pltpu.VMEM((1, BLK), jnp.int32),
+            pltpu.SMEM((1, BLK), jnp.int32),
+            pltpu.VMEM((count, BLK, TILE), bf16),
+            pltpu.VMEM((count, BLK, TILE), bf16),
+            pltpu.VMEM((count, 1, BLK), jnp.int32),
             pltpu.VMEM((classes, count, BLK, TILE), bf16),
             pltpu.VMEM((count, 1, BLK), jnp.int32),
             pltpu.SMEM((count, 1, BLK), jnp.int32),
@@ -416,9 +464,10 @@
             pltpu.VMEM((BLK, columns_dev), f32),
             pltpu.VMEM((count, columns_dev, BLK), bf16),
             pltpu.VMEM((pivots, columns_dev), f32),
+            pltpu.VMEM((4, columns_dev, 2 * TILE), f32),
             pltpu.VMEM((3, panel_width, panel_width), f32),
-            pltpu.VMEM((3, panel_width, panel_width), bf16),
-            pltpu.VMEM((3, panel_width, panel_width), bf16),
+            pltpu.VMEM((pivots, pivots), bf16),
+            pltpu.VMEM((pivots, pivots), bf16),
             pltpu.VMEM((units - 1, plane[0], plane[1], 8, columns_dev), f32),
             pltpu.VMEM((plane[1], plane[0], 8, columns_dev), f32),
             pltpu.VMEM((plane[0], 8, columns_dev), f32),
@@ -427,8 +476,7 @@
             pltpu.VMEM((plane[1] - 1, plane[0], 8, columns_dev), f32),
             pltpu.VMEM((units - 1, plane[1] - 1, 8, columns_dev), f32),
             pltpu.VMEM((plane[0] - 1, 8, columns_dev), f32),
-            dma((4,)),
-            dma,
+            dma((5,)),
             dma((2,)),
             dma((count,)),
             dma((count,)),
@@ -450,9 +498,18 @@
             dma((plane[0] - 1,)),
         ],
         compiler_params=pltpu.CompilerParams(
-            collective_id=0, has_side_effects=True, vmem_limit_bytes=48 * 1024 * 1024
+            collective_id=0, has_side_effects=True, vmem_limit_bytes=67043328
         ),
-    )(blocks, rows, parent_solution, front_rhs, coupling, inverse_one, inverse_two)
+    )(
+        live_counts,
+        parent_rows.reshape(count, BLK),
+        lower_panels.reshape(count, BLK, TILE),
+        parent_solution,
+        front_rhs,
+        coupling,
+        inverse_one,
+        inverse_two,
+    )
 
 
 def solution(mesh):

time: 90.7 us -> 82 us (0.904)
  local copies, waits for them, and re-layouts: 5.65 us -> 1.38 us
  Pallas kernels: 82.9 us -> 79.7 us
  other arithmetic: 0.97 us -> 0 us
    pallas_call x1, Pallas kernels: 82.9 us -> 79.7 us  [body(): pl.pallas_call(functools.partial(kernel, plane), out_shape=jax.ShapeDtype...]
    unnamed x11 -> x1, local copies, waits for them, and re-layouts: 3.5 us -> 1.38 us
    gather x2 -> x0, local copies, waits for them, and re-layouts: 1.32 us -> none  [the longest x1 0.75 us: body(): blocks = lower_panels.reshape(count, BLK, TILE)[block_of]]
where the time goes in v3:
time: 82 us; the launch traced here: 81.7 us
  Pallas kernels  79.7 us (97%)
  local copies, waits for them, and re-layouts  1.38 us (2%)
    pallas_call x1, Pallas kernels, body(): pl.pallas_call(functools.partial(kernel, plane), out_shape=jax.ShapeDtype...  79.7 us

profile of v3, /device:TPU:1, one launch (start us, length us, event | category | flops | bytes accessed | tf_op | source)
XLA Modules:
  0.0 81.7 jit_solution(695056328986740988)
XLA Ops:
  0.7 79.7 %shard_map.82 = f32[32,256]{1,0:T(8,128)} custom-call(s32[1]{0:T(128)S(6)} %copy.10.live_ref, s32[32,128]{1,0:T(8,128)} %bitcast.3, bf16[32,128,128]{2,1,0:T(8,128)(2,1)} %bitcast.2, bf16[4096,256]{1,0:T(8,128)(2,1)} %parent_ref.1, bf16[32,256]{1,0:T(8,128)(2,1)} %rhs_ref.1, f32[512,512]{1,0:T(8,128)} %coupling_hbm.1, f32[512,512]{1,0:T(8,128)} %inverse_one_hbm.1, ...), custom_call_target="tpu_custom_call" | custom-call | tf_op jit(solution)/shard_map/pallas_call | solution.py:448
  80.3 1.4 %copy.11 = f32[32,256]{1,0:T(8,128)} copy(f32[32,256]{1,0:T(8,128)} %shard_map.82) | data formatting | bytes 65536

commit v4 on v3

--- a/solution.py
+++ b/solution.py
@@ -12,6 +12,9 @@
 PLANE = (4, 8)
 RING = 4
 GROUP = 4
+BATCH = 2
+AHEAD = 2
+VMEM_BYTES = 66781184
 MESH = pl.DeviceIdType.MESH
 
 
@@ -158,18 +161,6 @@
     panels[side, 0] = blocks_ref[me]
     row_buf[0] = rows_ref[me]
 
-    loads[0].wait()
-    depth = staged.shape[0]
-    step = 256
-
-    def widen(i, carry):
-        at = pl.ds(pl.multiple_of(i * step, step), step)
-        wide[at, :] = staged[at, :].astype(jnp.float32)
-        return carry
-
-    lax.fori_loop(0, depth // step, widen, 0)
-    wide[depth:, :] = jnp.zeros((wide.shape[0] - depth, wide.shape[1]), jnp.float32)
-
     pl.semaphore_wait(barrier, count + 2)
 
     row_copies, blk_copies = [], []
@@ -184,6 +175,18 @@
         copy.start()
         blk_copies.append(copy)
 
+    loads[0].wait()
+    depth = staged.shape[0]
+    step = 256
+
+    def widen(i, carry):
+        at = pl.ds(pl.multiple_of(i * step, step), step)
+        wide[at, :] = staged[at, :].astype(jnp.float32)
+        return carry
+
+    lax.fori_loop(0, depth // step, widen, 0)
+    wide[depth:, :] = jnp.zeros((wide.shape[0] - depth, wide.shape[1]), jnp.float32)
+
     def part(cls, g):
         return panels.at[cls, pl.ds(g * GROUP, GROUP)]
 
@@ -195,8 +198,15 @@
         other = right if g % 2 == 0 else left
         return remote(part(cls, g), part(cls, g), far_send.at[g], far_recv.at[g], rhs=other)
 
-    def pair(slot, cls, g):
-        return remote(part(cls, g), part(cls, g), twin_send.at[slot, g], twin_recv.at[slot, g], rhs=twin)
+    def batch(cls, b):
+        return panels.at[cls, pl.ds(b * BATCH * GROUP, BATCH * GROUP)]
+
+    def pair(slot, cls, b):
+        return remote(batch(cls, b), batch(cls, b), twin_send.at[slot, b], twin_recv.at[slot, b], rhs=twin)
+
+    def share_twin(slot, cls, g):
+        if (g + 1) % BATCH == 0:
+            pair(slot, cls, g // BATCH).start()
 
     def take_rows():
         for copy in row_copies:
@@ -233,31 +243,32 @@
                 blk_copies[t - 1].wait_recv()
         near(0, side, g).start()
         near(1, side, g).start()
-        pair(0, side, g).start()
+        share_twin(0, side, g)
 
     def from_side(g):
         near(0, left, g).wait_recv()
-        pair(1, left, g).start()
+        share_twin(1, left, g)
         near(1, right, g).wait_recv()
-        pair(2, right, g).start()
+        share_twin(2, right, g)
 
     def relay(g):
         far(left if g % 2 == 0 else right, g).start()
 
     def from_far(g):
         far(opposite, g).wait_recv()
-        pair(3, opposite, g).start()
-
-    def term(slot, g):
+        share_twin(3, opposite, g)
+
+    def term(slot, b):
         chip = chips[slot]
-        pair(slot, chip * 2 + (1 - core), g).wait_recv()
-        at = pl.ds(g * GROUP, GROUP)
-        lhs = jnp.concatenate([fetched[g * GROUP + k] for k in range(GROUP)], axis=1)
+        pair(slot, chip * 2 + (1 - core), b).wait_recv()
+        size = BATCH * GROUP
+        at = pl.ds(b * size, size)
+        lhs = jnp.concatenate([fetched[b * size + k] for k in range(size)], axis=1)
         rhs = jnp.concatenate(
-            [panels[chip * 2 + c, at].reshape(GROUP * BLK, TILE) for c in range(2)], axis=1
+            [panels[chip * 2 + c, at].reshape(size * BLK, TILE) for c in range(2)], axis=1
         )
         value = jnp.dot(lhs, rhs, preferred_element_type=jnp.float32)
-        partial[slot] = value if g == 0 else partial[slot] + value
+        partial[slot] = value if b == 0 else partial[slot] + value
 
     def put(rows, columns, value):
         top, bottom = split(value)
@@ -284,20 +295,22 @@
             high[lower, upper] = jnp.zeros((half, half), jnp.bfloat16)
             low[lower, upper] = jnp.zeros((half, half), jnp.bfloat16)
 
+    ahead = min(AHEAD, groups - 3)
     for g in range(groups + 4):
         if g == groups - 1:
-            relay(0)
-            relay(1)
+            for k in range(ahead):
+                relay(k)
         if g < groups:
             forward(g)
         if g == 1:
             take_rows()
         if 2 <= g < groups + 2:
             from_side(g - 2)
-        if g >= groups:
-            for k in range(2 if g == groups else groups - 2 if g == groups + 1 else groups,
-                           groups - 2 if g == groups else groups if g == groups + 1 else groups):
+        if g == groups:
+            for k in range(ahead, groups - 1):
                 relay(k)
+        if g == groups + 1:
+            relay(groups - 1)
         if 1 <= g <= groups:
             gather_group(g - 1)
         if g == groups - 4:
@@ -306,11 +319,11 @@
             invert(1)
         if g == groups - 2:
             invert(2)
-        if 3 <= g < groups + 3:
-            term(0, g - 3)
-        if g >= 4:
-            term(1, g - 4)
-            term(2, g - 4)
+        if 3 <= g < groups + 3 and (g - 2) % BATCH == 0:
+            term(0, (g - 3) // BATCH)
+        if g >= 4 and (g - 3) % BATCH == 0:
+            term(1, (g - 4) // BATCH)
+            term(2, (g - 4) // BATCH)
 
     def pivots(slot):
         return pl.ds(pl.multiple_of(chips[slot] * width, width), width)
@@ -324,13 +337,14 @@
     product[pivots(3), :] = jnp.zeros((width, acc_cols), jnp.float32)
     product[own, :] = product[own, :] + rhs_ref[...].astype(jnp.float32)
     product[...] = dot_split((high[...], low[...]), split(product[...]))
-    for g in range(groups // 2):
-        term(3, g)
+    batches = groups // BATCH
+    for b in range(batches // 2):
+        term(3, b)
     for g in range(groups // 2, groups):
         from_far(g)
-        if g > groups // 2:
-            term(3, g - 1)
-    term(3, groups - 1)
+        if g >= groups // 2 + BATCH and g % BATCH == BATCH - 1:
+            term(3, g // BATCH - 1)
+    term(3, batches - 1)
 
     units = share // 8
     stripes = units - 1
@@ -417,8 +431,9 @@
         near(0, side, g).wait_send()
         near(1, side, g).wait_send()
         far(left if g % 2 == 0 else right, g).wait_send()
-        for slot, cls in enumerate((side, left, right, opposite)):
-            pair(slot, cls, g).wait_send()
+    for slot, cls in enumerate((side, left, right, opposite)):
+        for b in range(batches):
+            pair(slot, cls, b).wait_send()
 
 
 def body(
@@ -486,8 +501,8 @@
             dma((2, groups)),
             dma((groups,)),
             dma((groups,)),
-            dma((4, groups)),
-            dma((4, groups)),
+            dma((4, groups // BATCH)),
+            dma((4, groups // BATCH)),
             dma((units - 1, plane[0] - 1)),
             dma((units - 1, plane[0] - 1)),
             dma((plane[1] - 1,)),
@@ -498,7 +513,7 @@
             dma((plane[0] - 1,)),
         ],
         compiler_params=pltpu.CompilerParams(
-            collective_id=0, has_side_effects=True, vmem_limit_bytes=67043328
+            collective_id=0, has_side_effects=True, vmem_limit_bytes=VMEM_BYTES
         ),
     )(
         live_counts,

time: 82 us -> 80.7 us (0.984)
  Pallas kernels: 79.7 us -> 78.4 us
    pallas_call x1, Pallas kernels: 79.7 us -> 78.4 us  [body(): pl.pallas_call(functools.partial(kernel, plane), out_shape=jax.ShapeDtype...]
where the time goes in v4:
time: 80.7 us; the launch traced here: 80.4 us
  Pallas kernels  78.4 us (97%)
  local copies, waits for them, and re-layouts  1.38 us (2%)
    pallas_call x1, Pallas kernels, body(): pl.pallas_call(functools.partial(kernel, plane), out_shape=jax.ShapeDtype...  78.4 us

profile of v4, /device:TPU:1, one launch (start us, length us, event | category | flops | bytes accessed | tf_op | source)
XLA Modules:
  0.0 80.4 jit_solution(1005102129334492098)
XLA Ops:
  0.7 78.4 %shard_map.82 = f32[32,256]{1,0:T(8,128)} custom-call(s32[1]{0:T(128)S(6)} %copy.10.live_ref, s32[32,128]{1,0:T(8,128)} %bitcast.3, bf16[32,128,128]{2,1,0:T(8,128)(2,1)} %bitcast.2, bf16[4096,256]{1,0:T(8,128)(2,1)} %parent_ref.1, bf16[32,256]{1,0:T(8,128)(2,1)} %rhs_ref.1, f32[512,512]{1,0:T(8,128)} %coupling_hbm.1, f32[512,512]{1,0:T(8,128)} %inverse_one_hbm.1, ...), custom_call_target="tpu_custom_call" | custom-call | tf_op jit(solution)/shard_map/pallas_call | solution.py:463
  79.0 1.4 %copy.11 = f32[32,256]{1,0:T(8,128)} copy(f32[32,256]{1,0:T(8,128)} %shard_map.82) | data formatting | bytes 65536

commit v5 on v4

--- a/solution.py
+++ b/solution.py
@@ -63,6 +63,7 @@
     picked,
     fetched,
     product,
+    answer,
     partial,
     matrices,
     high,
@@ -295,6 +296,15 @@
             high[lower, upper] = jnp.zeros((half, half), jnp.bfloat16)
             low[lower, upper] = jnp.zeros((half, half), jnp.bfloat16)
 
+    share = rhs_ref.shape[0]
+
+    def pivots(slot):
+        return pl.ds(pl.multiple_of(chips[slot] * width, width), width)
+
+    def solved(slot):
+        value = product[pivots(slot), :] - partial[slot].T
+        return dot_split((high[:, pivots(slot)], low[:, pivots(slot)]), split(value))
+
     ahead = min(AHEAD, groups - 3)
     for g in range(groups + 4):
         if g == groups - 1:
@@ -315,6 +325,9 @@
             gather_group(g - 1)
         if g == groups - 4:
             invert(0)
+            product[...] = jnp.zeros_like(product)
+            own = pl.ds(pl.multiple_of(me * share, share), share)
+            product[own, :] = rhs_ref[...].astype(jnp.float32)
         if g == groups - 3:
             invert(1)
         if g == groups - 2:
@@ -325,35 +338,28 @@
             term(1, (g - 4) // BATCH)
             term(2, (g - 4) // BATCH)
 
-    def pivots(slot):
-        return pl.ds(pl.multiple_of(chips[slot] * width, width), width)
-
-    for g in range(groups // 2):
+    batches = groups // BATCH
+    from_far(0)
+    answer[...] = solved(0)
+    from_far(1)
+    answer[...] = answer[...] + solved(1)
+    from_far(2)
+    from_far(3)
+    answer[...] = answer[...] + solved(2)
+    for g in range(4, groups):
         from_far(g)
-    share = rhs_ref.shape[0]
-    own = pl.ds(pl.multiple_of(me * share, share), share)
-    for slot in range(3):
-        product[pivots(slot), :] = -partial[slot].T
-    product[pivots(3), :] = jnp.zeros((width, acc_cols), jnp.float32)
-    product[own, :] = product[own, :] + rhs_ref[...].astype(jnp.float32)
-    product[...] = dot_split((high[...], low[...]), split(product[...]))
-    batches = groups // BATCH
-    for b in range(batches // 2):
-        term(3, b)
-    for g in range(groups // 2, groups):
-        from_far(g)
-        if g >= groups // 2 + BATCH and g % BATCH == BATCH - 1:
-            term(3, g // BATCH - 1)
+        if g % BATCH == 0:
+            term(3, g // BATCH - 2)
+    term(3, batches - 2)
     term(3, batches - 1)
 
     units = share // 8
     stripes = units - 1
-    last = dot_split((high[:, pivots(3)], low[:, pivots(3)]), split(-partial[3].T))
-    answer = product[...] + last
+    total = answer[...] + solved(3)
     for r in range(count):
         index_y, index_z = divmod(r, size_z)
         for u in range(units):
-            rows = answer[r * share + u * 8 : r * share + u * 8 + 8]
+            rows = total[r * share + u * 8 : r * share + u * 8 + 8]
             if u < stripes:
                 first_y[u, index_y, index_z] = rows
             else:
@@ -478,6 +484,7 @@
             pltpu.VMEM((rows_dev + 8, columns_dev), f32),
             pltpu.VMEM((BLK, columns_dev), f32),
             pltpu.VMEM((count, columns_dev, BLK), bf16),
+            pltpu.VMEM((pivots, columns_dev), f32),
             pltpu.VMEM((pivots, columns_dev), f32),
             pltpu.VMEM((4, columns_dev, 2 * TILE), f32),
             pltpu.VMEM((3, panel_width, panel_width), f32),

time: 80.7 us -> 79.6 us (0.986)
  Pallas kernels: 78.4 us -> 77.3 us
    pallas_call x1, Pallas kernels: 78.4 us -> 77.3 us  [body(): pl.pallas_call(functools.partial(kernel, plane), out_shape=jax.ShapeDtype...]
where the time goes in v5:
time: 79.6 us; the launch traced here: 79.3 us
  Pallas kernels  77.3 us (97%)
  local copies, waits for them, and re-layouts  1.38 us (2%)
    pallas_call x1, Pallas kernels, body(): pl.pallas_call(functools.partial(kernel, plane), out_shape=jax.ShapeDtype...  77.3 us

profile of v5, /device:TPU:1, one launch (start us, length us, event | category | flops | bytes accessed | tf_op | source)
XLA Modules:
  0.0 79.3 jit_solution(18253712340990191587)
XLA Ops:
  0.7 77.3 %shard_map.82 = f32[32,256]{1,0:T(8,128)} custom-call(s32[1]{0:T(128)S(6)} %copy.10.live_ref, s32[32,128]{1,0:T(8,128)} %bitcast.3, bf16[32,128,128]{2,1,0:T(8,128)(2,1)} %bitcast.2, bf16[4096,256]{1,0:T(8,128)(2,1)} %parent_ref.1, bf16[32,256]{1,0:T(8,128)(2,1)} %rhs_ref.1, f32[512,512]{1,0:T(8,128)} %coupling_hbm.1, f32[512,512]{1,0:T(8,128)} %inverse_one_hbm.1, ...), custom_call_target="tpu_custom_call" | custom-call | tf_op jit(solution)/shard_map/pallas_call | solution.py:469
  77.9 1.4 %copy.11 = f32[32,256]{1,0:T(8,128)} copy(f32[32,256]{1,0:T(8,128)} %shard_map.82) | data formatting | bytes 65536

commit v6 on v5

--- a/solution.py
+++ b/solution.py
@@ -14,7 +14,7 @@
 GROUP = 4
 BATCH = 2
 AHEAD = 2
-VMEM_BYTES = 66781184
+VMEM_BYTES = 56000000
 MESH = pl.DeviceIdType.MESH
 
 

time: 79.6 us -> 78.7 us (0.989)
  Pallas kernels: 77.3 us -> 75.7 us
    pallas_call x1, Pallas kernels: 77.3 us -> 75.7 us  [body(): pl.pallas_call(functools.partial(kernel, plane), out_shape=jax.ShapeDtype...]
    unnamed x1 -> x5, local copies, waits for them, and re-layouts: 1.38 us -> 2.04 us
where the time goes in v6:
time: 78.7 us; the launch traced here: 78.4 us
  Pallas kernels  75.7 us (96%)
  local copies, waits for them, and re-layouts  2.04 us (3%)
    pallas_call x1, Pallas kernels, body(): pl.pallas_call(functools.partial(kernel, plane), out_shape=jax.ShapeDtype...  75.7 us
    unnamed x5, local copies, waits for them, and re-layouts  2.04 us

profile of v6, /device:TPU:1, one launch (start us, length us, event | category | flops | bytes accessed | tf_op | source)
XLA Modules:
  0.0 78.4 jit_solution(1409720508892794344)
XLA Ops:
  0.7 0.0 copy-start
  0.7 0.7 copy-done
  1.4 0.0 copy-start.1
  1.4 0.7 copy-done.1
  2.1 75.7 %shard_map.82 = f32[32,256]{1,0:T(8,128)S(1)} custom-call(s32[1]{0:T(128)S(6)} %copy.10.live_ref, s32[32,128]{1,0:T(8,128)S(1)} %bitcast.2, bf16[32,128,128]{2,1,0:T(8,128)(2,1)} %bitcast.3, bf16[4096,256]{1,0:T(8,128)(2,1)} %parent_ref.1, bf16[32,256]{1,0:T(8,128)(2,1)S(1)} %copy-done.1, f32[512,512]{1,0:T(8,128)} %coupling_hbm.1, ...), custom_call_target="tpu_custom_call" | custom-call | tf_op jit(solution)/shard_map/pallas_call | solution.py:469
  77.8 0.6 copy.11
Async XLA Ops:
  0.7 0.7 copy-start
  1.4 0.7 copy-start.1

commit v7 on v6

--- a/solution.py
+++ b/solution.py
@@ -14,6 +14,8 @@
 GROUP = 4
 BATCH = 2
 AHEAD = 2
+INVAT = 4
+ZFIRST = 1
 VMEM_BYTES = 56000000
 MESH = pl.DeviceIdType.MESH
 
@@ -323,14 +325,14 @@
             relay(groups - 1)
         if 1 <= g <= groups:
             gather_group(g - 1)
-        if g == groups - 4:
+        if g == INVAT:
             invert(0)
             product[...] = jnp.zeros_like(product)
             own = pl.ds(pl.multiple_of(me * share, share), share)
             product[own, :] = rhs_ref[...].astype(jnp.float32)
-        if g == groups - 3:
+        if g == INVAT + 1:
             invert(1)
-        if g == groups - 2:
+        if g == INVAT + 2:
             invert(2)
         if 3 <= g < groups + 3 and (g - 2) % BATCH == 0:
             term(0, (g - 3) // BATCH)
@@ -366,6 +368,18 @@
                 first_z[index_z, index_y] = rows
 
     y_copies, z_copies, yz_copies, zy_copies = [], [], [], []
+    def start_z():
+        for dz in range(1, size_z):
+            to = (z + size_z - dz) % size_z
+            copy = remote(
+                first_z.at[to], got_z.at[dz - 1], z_send.at[dz - 1], z_recv.at[dz - 1],
+                rows=y * size_z + to,
+            )
+            copy.start()
+            z_copies.append(copy)
+
+    if ZFIRST:
+        start_z()
     for u in range(stripes):
         for dy in range(1, size_y):
             to = (y + size_y - dy) % size_y
@@ -375,15 +389,8 @@
             )
             copy.start()
             y_copies.append(copy)
-        if u == 0:
-            for dz in range(1, size_z):
-                to = (z + size_z - dz) % size_z
-                copy = remote(
-                    first_z.at[to], got_z.at[dz - 1], z_send.at[dz - 1], z_recv.at[dz - 1],
-                    rows=y * size_z + to,
-                )
-                copy.start()
-                z_copies.append(copy)
+        if u == 0 and not ZFIRST:
+            start_z()
 
     def reduce_y(u):
         total = first_y[u, y]

time: 78.7 us -> 78.8 us (level)
  no operation moved by 1% of the time
where the time goes in v7:
time: 78.8 us; the launch traced here: 78.5 us
  Pallas kernels  75.8 us (96%)
  local copies, waits for them, and re-layouts  2.04 us (3%)
    pallas_call x1, Pallas kernels, body(): pl.pallas_call(functools.partial(kernel, plane), out_shape=jax.ShapeDtype...  75.8 us
    unnamed x5, local copies, waits for them, and re-layouts  2.04 us

profile of v7, /device:TPU:1, one launch (start us, length us, event | category | flops | bytes accessed | tf_op | source)
XLA Modules:
  0.0 78.5 jit_solution(6121554471978235772)
XLA Ops:
  0.7 0.0 copy-start
  0.7 0.7 copy-done
  1.4 0.0 copy-start.1
  1.4 0.7 copy-done.1
  2.1 75.8 %shard_map.82 = f32[32,256]{1,0:T(8,128)S(1)} custom-call(s32[1]{0:T(128)S(6)} %copy.10.live_ref, s32[32,128]{1,0:T(8,128)S(1)} %bitcast.2, bf16[32,128,128]{2,1,0:T(8,128)(2,1)} %bitcast.3, bf16[4096,256]{1,0:T(8,128)(2,1)} %parent_ref.1, bf16[32,256]{1,0:T(8,128)(2,1)S(1)} %copy-done.1, f32[512,512]{1,0:T(8,128)} %coupling_hbm.1, ...), custom_call_target="tpu_custom_call" | custom-call | tf_op jit(solution)/shard_map/pallas_call | solution.py:476
  77.9 0.6 copy.11
Async XLA Ops:
  0.7 0.7 copy-start
  1.4 0.7 copy-start.1
